TPU v7x, 32 devices: a whole 2x2x4 slice. The times are simulated.
32 devices in a mesh: expert: 8 (over y, x, core), token: 4 (over z).
Axes of the slice: x: 2, y: 2, z: 4, core: 2. Of those that a mesh axis runs over, the one named last changes fastest.
Arguments:
- activations: bfloat16 [16, 1024, 768], P('expert', 'token'), may hold values from -6 to 6
- routed: int32 [16, 1024], P('expert', 'token'), may hold values 0 or 1
- weights: bfloat16 [128, 768, 256], P(('expert', 'token')), may hold values from -6 to 6, as said below
- kept_mask: int32 [128, 768, 256], P(('expert', 'token')), may hold values 0 or 1
- step_counts: int32 [128], P(('expert', 'token')), may hold values from 1 to 7
- ridge_scale: float32 [128], P(('expert', 'token')), may hold values from 0.05 to 0.5
Outputs:
- rebuilt: float32 [128, 768, 256], P(('expert', 'token'))
- misfit: float32 [16], P('expert')
Inputs may be any that keep to these rules, and one draw needn't show every extreme that they name: `weights`: every entry's magnitude is at least 0.25.
All inputs are finite; a program needn't handle non-finite values. No bound on the sum of `routed` or of `kept_mask` on one device may be relied on, other than what follows from the above.
Results may differ from a plain program's by a relative error of at most 0.0003.
Values may be sent and summed in bfloat16 or wider, within the bound.
A program may use at most 64 MiB of HBM per device.

v0:
```python
import jax
import jax.numpy as jnp
from jax import lax
from jax.sharding import PartitionSpec as P

D = 2048
COLS = 256


def solve_task(gram_matrix, frobenius, task_weights, task_mask, task_count, task_ridge):
    float_weights = task_weights.astype(jnp.float32)
    float_mask = task_mask.astype(jnp.float32)
    damping = task_ridge * frobenius
    step_size = 1.0 / (frobenius + damping)

    def advance(turn_index, current):
        gradient = (
            jnp.dot(gram_matrix, current - float_weights, precision=lax.Precision.HIGHEST)
            + damping * current
        )
        return current - step_size * (float_mask * gradient)

    result = lax.fori_loop(0, task_count, advance, float_mask * float_weights)
    change = result - float_weights
    numerator = jnp.sum(change * jnp.dot(gram_matrix, change, precision=lax.Precision.HIGHEST))
    energy = jnp.sum(
        float_weights * jnp.dot(gram_matrix, float_weights, precision=lax.Precision.HIGHEST)
    )
    return (result, numerator, energy)


def on_device(activations, routed, weights, kept_mask, step_counts, ridge_scale):
    local_experts, row_count, features = activations.shape
    local_tasks = weights.shape[0]
    per_expert = D // COLS
    total_rows = row_count * lax.axis_size("token")
    own_slot = lax.axis_index("token") * local_tasks // per_expert
    masked = activations * routed[:, :, None].astype(jnp.bfloat16)
    own_rows = lax.dynamic_index_in_dim(
        lax.all_gather(masked, "token", axis=1, tiled=True), own_slot, 0, keepdims=False
    )
    gram_sum = lax.dot_general(
        own_rows, own_rows, (((0,), (0,)), ((), ())), preferred_element_type=jnp.float32
    )
    gram_matrix = gram_sum / total_rows
    frobenius = jnp.sqrt(jnp.sum(gram_matrix * gram_matrix))

    def one_task(task_args):
        task_weights, task_mask, task_count, task_ridge = task_args
        return solve_task(gram_matrix, frobenius, task_weights, task_mask, task_count, task_ridge)

    rebuilt, numerators, energies = lax.map(
        one_task, (weights, kept_mask, step_counts, ridge_scale)
    )
    picker = (jnp.arange(local_experts) == own_slot).astype(jnp.float32)
    expert_terms = lax.psum(picker * jnp.sum(numerators), "token")
    layer_energy = lax.psum(jnp.sum(energies), ("expert", "token"))
    expert_total = local_experts * lax.axis_size("expert")
    misfit = expert_terms / (layer_energy / expert_total + 1e-06)
    return (rebuilt, misfit)


def solution(mesh):
    placed = (
        P("expert", "token", None),
        P("expert", "token"),
        P(("expert", "token"), None, None),
        P(("expert", "token"), None, None),
        P(("expert", "token")),
        P(("expert", "token")),
    )
    return jax.shard_map(
        on_device,
        mesh=mesh,
        in_specs=placed,
        out_specs=(P(("expert", "token"), None, None), P("expert")),
        check_vma=False,
    )
```

profile of v0, /device:TPU:0, one launch (start us, length us, event | category | flops | bytes accessed | tf_op | source)
XLA Modules:
  0.0 320.7 jit_solution(10718532296523301616)
XLA Ops:
  10.2 66.2 %all-gather.2.cloned.1.call-done = bf16[2,1024,768]{2,1,0:T(8,128)(2,1)} async-done(((bf16[2,256,768]{2,1,0:T(8,128)(2,1)}), bf16[2,1024,768]{2,1,0:T(8,128)(2,1)}) %all-gather.2.cloned.1.call-update) | async-done | bytes 3145744 | tf_op jit(solution)/shard_map/all_gather | solution.py:40
  76.4 4.1 %multiply_reduce_fusion = (f32[]{:T(128)}, f32[768,768]{1,0:T(8,128)S(1)}) fusion(bf16[2,1024,768]{2,1,0:T(8,128)(2,1)} %all-gather.2.cloned.1.call-done, s32[]{:T(128)S(6)} %select_n.10), kind=kOutput, calls=%fused_computation.22 | convolution fusion | flops 1209729024 | bytes 3932168 | tf_op jit(solution)/shard_map/dot_general | solution.py:42
  81.1 163.0 %while.25 = (s32[]{:T(128)}, f32[4,768,256]{2,1,0:T(8,128)}, f32[4]{0:T(128)S(1)}, f32[4]{0:T(128)S(1)}, s32[4,768,256]{2,1,0:T(8,128)}, /*index=5*/bf16[4,768,2...) while((s32[]{:T(128)}, f32[4,768,256]{2,1,0:T(8,128)}, ...), condition=%wide.region_6.7_spmd, body=%wide.region_1.6_spmd.sunk | while | flops 5439750144 | bytes 29491652 | solution.py:52
  84.1 2.2 fusion.35
  94.6 27.0 %while.26 = (s32[]{:T(128)}, f32[768,256]{0,1:T(8,128)S(1)}, s32[]{:T(128)}, f32[]{:T(128)}, f32[768,256]{0,1:T(8,128)}, /*index=5*/f32[768,768]{1,0:T(8,128)S(1)}, f32[]{:T(128)}, f32[768,256]{0,1:T(8,128)}, s32[]{:T(128)}) while((s32[]{:T(128)}, f32[768,256]{0,1:T(8,128)S(1)}, s32[]{:T(128)}, f32[]{:T(128)}, f32[768,256]{0,1:T(8,128)}, ...), condition=%wide.region_3.3_spmd, body=%wide.region_2.2_spmd.sunk | while | flops 1813118976 | bytes 7077989 | solution.py:23
  95.3 3.7 %fusion.38 = f32[768,256]{0,1:T(8,128)S(1)} fusion(f32[768,256]{0,1:T(8,128)S(1)} %copy.48, f32[768,256]{0,1:T(8,128)} %get-tuple-element.307, f32[768,768]{1,0:T(8,128)S(1)} %get-tuple-element.305, f32[768,256]{0,1:T(8,128)} %get-tuple-element.304, f32[]{:T(128)} %get-tuple-element.306, f32[]{:T(128)} %get-tuple-element.303), kind=kOutput, calls=%fused_computation.4.clone.1 | convolution fusion | flops 1813118976 | bytes 5505032 | tf_op jit(solution)/shard_map/while/body/eval_jaxpr/while/body/dot_general | solution.py:18
  99.7 3.7 %fusion.38 = f32[768,256]{0,1:T(8,128)S(1)} fusion(f32[768,256]{0,1:T(8,128)S(1)} %copy.48, f32[768,256]{0,1:T(8,128)} %get-tuple-element.307, f32[768,768]{1,0:T(8,128)S(1)} %get-tuple-element.305, f32[768,256]{0,1:T(8,128)} %get-tuple-element.304, f32[]{:T(128)} %get-tuple-element.306, f32[]{:T(128)} %get-tuple-element.303), kind=kOutput, calls=%fused_computation.4.clone.1 | convolution fusion | flops 1813118976 | bytes 5505032 | tf_op jit(solution)/shard_map/while/body/eval_jaxpr/while/body/dot_general | solution.py:18
  104.1 3.7 %fusion.38 = f32[768,256]{0,1:T(8,128)S(1)} fusion(f32[768,256]{0,1:T(8,128)S(1)} %copy.48, f32[768,256]{0,1:T(8,128)} %get-tuple-element.307, f32[768,768]{1,0:T(8,128)S(1)} %get-tuple-element.305, f32[768,256]{0,1:T(8,128)} %get-tuple-element.304, f32[]{:T(128)} %get-tuple-element.306, f32[]{:T(128)} %get-tuple-element.303), kind=kOutput, calls=%fused_computation.4.clone.1 | convolution fusion | flops 1813118976 | bytes 5505032 | tf_op jit(solution)/shard_map/while/body/eval_jaxpr/while/body/dot_general | solution.py:18
  108.5 3.7 %fusion.38 = f32[768,256]{0,1:T(8,128)S(1)} fusion(f32[768,256]{0,1:T(8,128)S(1)} %copy.48, f32[768,256]{0,1:T(8,128)} %get-tuple-element.307, f32[768,768]{1,0:T(8,128)S(1)} %get-tuple-element.305, f32[768,256]{0,1:T(8,128)} %get-tuple-element.304, f32[]{:T(128)} %get-tuple-element.306, f32[]{:T(128)} %get-tuple-element.303), kind=kOutput, calls=%fused_computation.4.clone.1 | convolution fusion | flops 1813118976 | bytes 5505032 | tf_op jit(solution)/shard_map/while/body/eval_jaxpr/while/body/dot_general | solution.py:18
  112.9 3.7 %fusion.38 = f32[768,256]{0,1:T(8,128)S(1)} fusion(f32[768,256]{0,1:T(8,128)S(1)} %copy.48, f32[768,256]{0,1:T(8,128)} %get-tuple-element.307, f32[768,768]{1,0:T(8,128)S(1)} %get-tuple-element.305, f32[768,256]{0,1:T(8,128)} %get-tuple-element.304, f32[]{:T(128)} %get-tuple-element.306, f32[]{:T(128)} %get-tuple-element.303), kind=kOutput, calls=%fused_computation.4.clone.1 | convolution fusion | flops 1813118976 | bytes 5505032 | tf_op jit(solution)/shard_map/while/body/eval_jaxpr/while/body/dot_general | solution.py:18
  117.3 3.7 %fusion.38 = f32[768,256]{0,1:T(8,128)S(1)} fusion(f32[768,256]{0,1:T(8,128)S(1)} %copy.48, f32[768,256]{0,1:T(8,128)} %get-tuple-element.307, f32[768,768]{1,0:T(8,128)S(1)} %get-tuple-element.305, f32[768,256]{0,1:T(8,128)} %get-tuple-element.304, f32[]{:T(128)} %get-tuple-element.306, f32[]{:T(128)} %get-tuple-element.303), kind=kOutput, calls=%fused_computation.4.clone.1 | convolution fusion | flops 1813118976 | bytes 5505032 | tf_op jit(solution)/shard_map/while/body/eval_jaxpr/while/body/dot_general | solution.py:18
  121.6 2.9 fusion.34
  142.0 27.0 %while.26 = (s32[]{:T(128)}, f32[768,256]{0,1:T(8,128)S(1)}, s32[]{:T(128)}, f32[]{:T(128)}, f32[768,256]{0,1:T(8,128)}, /*index=5*/f32[768,768]{1,0:T(8,128)S(1)}, f32[]{:T(128)}, f32[768,256]{0,1:T(8,128)}, s32[]{:T(128)}) while((s32[]{:T(128)}, f32[768,256]{0,1:T(8,128)S(1)}, s32[]{:T(128)}, f32[]{:T(128)}, f32[768,256]{0,1:T(8,128)}, ...), condition=%wide.region_3.3_spmd, body=%wide.region_2.2_spmd.sunk | while | flops 1813118976 | bytes 7077989 | solution.py:23
  142.7 3.7 %fusion.38 = f32[768,256]{0,1:T(8,128)S(1)} fusion(f32[768,256]{0,1:T(8,128)S(1)} %copy.48, f32[768,256]{0,1:T(8,128)} %get-tuple-element.307, f32[768,768]{1,0:T(8,128)S(1)} %get-tuple-element.305, f32[768,256]{0,1:T(8,128)} %get-tuple-element.304, f32[]{:T(128)} %get-tuple-element.306, f32[]{:T(128)} %get-tuple-element.303), kind=kOutput, calls=%fused_computation.4.clone.1 | convolution fusion | flops 1813118976 | bytes 5505032 | tf_op jit(solution)/shard_map/while/body/eval_jaxpr/while/body/dot_general | solution.py:18
  147.1 3.7 %fusion.38 = f32[768,256]{0,1:T(8,128)S(1)} fusion(f32[768,256]{0,1:T(8,128)S(1)} %copy.48, f32[768,256]{0,1:T(8,128)} %get-tuple-element.307, f32[768,768]{1,0:T(8,128)S(1)} %get-tuple-element.305, f32[768,256]{0,1:T(8,128)} %get-tuple-element.304, f32[]{:T(128)} %get-tuple-element.306, f32[]{:T(128)} %get-tuple-element.303), kind=kOutput, calls=%fused_computation.4.clone.1 | convolution fusion | flops 1813118976 | bytes 5505032 | tf_op jit(solution)/shard_map/while/body/eval_jaxpr/while/body/dot_general | solution.py:18
  151.5 3.7 %fusion.38 = f32[768,256]{0,1:T(8,128)S(1)} fusion(f32[768,256]{0,1:T(8,128)S(1)} %copy.48, f32[768,256]{0,1:T(8,128)} %get-tuple-element.307, f32[768,768]{1,0:T(8,128)S(1)} %get-tuple-element.305, f32[768,256]{0,1:T(8,128)} %get-tuple-element.304, f32[]{:T(128)} %get-tuple-element.306, f32[]{:T(128)} %get-tuple-element.303), kind=kOutput, calls=%fused_computation.4.clone.1 | convolution fusion | flops 1813118976 | bytes 5505032 | tf_op jit(solution)/shard_map/while/body/eval_jaxpr/while/body/dot_general | solution.py:18
  155.8 3.7 %fusion.38 = f32[768,256]{0,1:T(8,128)S(1)} fusion(f32[768,256]{0,1:T(8,128)S(1)} %copy.48, f32[768,256]{0,1:T(8,128)} %get-tuple-element.307, f32[768,768]{1,0:T(8,128)S(1)} %get-tuple-element.305, f32[768,256]{0,1:T(8,128)} %get-tuple-element.304, f32[]{:T(128)} %get-tuple-element.306, f32[]{:T(128)} %get-tuple-element.303), kind=kOutput, calls=%fused_computation.4.clone.1 | convolution fusion | flops 1813118976 | bytes 5505032 | tf_op jit(solution)/shard_map/while/body/eval_jaxpr/while/body/dot_general | solution.py:18
  160.2 3.7 %fusion.38 = f32[768,256]{0,1:T(8,128)S(1)} fusion(f32[768,256]{0,1:T(8,128)S(1)} %copy.48, f32[768,256]{0,1:T(8,128)} %get-tuple-element.307, f32[768,768]{1,0:T(8,128)S(1)} %get-tuple-element.305, f32[768,256]{0,1:T(8,128)} %get-tuple-element.304, f32[]{:T(128)} %get-tuple-element.306, f32[]{:T(128)} %get-tuple-element.303), kind=kOutput, calls=%fused_computation.4.clone.1 | convolution fusion | flops 1813118976 | bytes 5505032 | tf_op jit(solution)/shard_map/while/body/eval_jaxpr/while/body/dot_general | solution.py:18
  164.6 3.7 %fusion.38 = f32[768,256]{0,1:T(8,128)S(1)} fusion(f32[768,256]{0,1:T(8,128)S(1)} %copy.48, f32[768,256]{0,1:T(8,128)} %get-tuple-element.307, f32[768,768]{1,0:T(8,128)S(1)} %get-tuple-element.305, f32[768,256]{0,1:T(8,128)} %get-tuple-element.304, f32[]{:T(128)} %get-tuple-element.306, f32[]{:T(128)} %get-tuple-element.303), kind=kOutput, calls=%fused_computation.4.clone.1 | convolution fusion | flops 1813118976 | bytes 5505032 | tf_op jit(solution)/shard_map/while/body/eval_jaxpr/while/body/dot_general | solution.py:18
  168.9 2.9 fusion.34
  189.3 13.8 %while.26 = (s32[]{:T(128)}, f32[768,256]{0,1:T(8,128)S(1)}, s32[]{:T(128)}, f32[]{:T(128)}, f32[768,256]{0,1:T(8,128)}, /*index=5*/f32[768,768]{1,0:T(8,128)S(1)}, f32[]{:T(128)}, f32[768,256]{0,1:T(8,128)}, s32[]{:T(128)}) while((s32[]{:T(128)}, f32[768,256]{0,1:T(8,128)S(1)}, s32[]{:T(128)}, f32[]{:T(128)}, f32[768,256]{0,1:T(8,128)}, ...), condition=%wide.region_3.3_spmd, body=%wide.region_2.2_spmd.sunk | while | flops 1813118976 | bytes 7077989 | solution.py:23
  190.0 3.7 %fusion.38 = f32[768,256]{0,1:T(8,128)S(1)} fusion(f32[768,256]{0,1:T(8,128)S(1)} %copy.48, f32[768,256]{0,1:T(8,128)} %get-tuple-element.307, f32[768,768]{1,0:T(8,128)S(1)} %get-tuple-element.305, f32[768,256]{0,1:T(8,128)} %get-tuple-element.304, f32[]{:T(128)} %get-tuple-element.306, f32[]{:T(128)} %get-tuple-element.303), kind=kOutput, calls=%fused_computation.4.clone.1 | convolution fusion | flops 1813118976 | bytes 5505032 | tf_op jit(solution)/shard_map/while/body/eval_jaxpr/while/body/dot_general | solution.py:18
  194.4 3.7 %fusion.38 = f32[768,256]{0,1:T(8,128)S(1)} fusion(f32[768,256]{0,1:T(8,128)S(1)} %copy.48, f32[768,256]{0,1:T(8,128)} %get-tuple-element.307, f32[768,768]{1,0:T(8,128)S(1)} %get-tuple-element.305, f32[768,256]{0,1:T(8,128)} %get-tuple-element.304, f32[]{:T(128)} %get-tuple-element.306, f32[]{:T(128)} %get-tuple-element.303), kind=kOutput, calls=%fused_computation.4.clone.1 | convolution fusion | flops 1813118976 | bytes 5505032 | tf_op jit(solution)/shard_map/while/body/eval_jaxpr/while/body/dot_general | solution.py:18
  198.8 3.7 %fusion.38 = f32[768,256]{0,1:T(8,128)S(1)} fusion(f32[768,256]{0,1:T(8,128)S(1)} %copy.48, f32[768,256]{0,1:T(8,128)} %get-tuple-element.307, f32[768,768]{1,0:T(8,128)S(1)} %get-tuple-element.305, f32[768,256]{0,1:T(8,128)} %get-tuple-element.304, f32[]{:T(128)} %get-tuple-element.306, f32[]{:T(128)} %get-tuple-element.303), kind=kOutput, calls=%fused_computation.4.clone.1 | convolution fusion | flops 1813118976 | bytes 5505032 | tf_op jit(solution)/shard_map/while/body/eval_jaxpr/while/body/dot_general | solution.py:18
  203.1 2.9 fusion.34
  223.5 13.8 %while.26 = (s32[]{:T(128)}, f32[768,256]{0,1:T(8,128)S(1)}, s32[]{:T(128)}, f32[]{:T(128)}, f32[768,256]{0,1:T(8,128)}, /*index=5*/f32[768,768]{1,0:T(8,128)S(1)}, f32[]{:T(128)}, f32[768,256]{0,1:T(8,128)}, s32[]{:T(128)}) while((s32[]{:T(128)}, f32[768,256]{0,1:T(8,128)S(1)}, s32[]{:T(128)}, f32[]{:T(128)}, f32[768,256]{0,1:T(8,128)}, ...), condition=%wide.region_3.3_spmd, body=%wide.region_2.2_spmd.sunk | while | flops 1813118976 | bytes 7077989 | solution.py:23
  224.2 3.7 %fusion.38 = f32[768,256]{0,1:T(8,128)S(1)} fusion(f32[768,256]{0,1:T(8,128)S(1)} %copy.48, f32[768,256]{0,1:T(8,128)} %get-tuple-element.307, f32[768,768]{1,0:T(8,128)S(1)} %get-tuple-element.305, f32[768,256]{0,1:T(8,128)} %get-tuple-element.304, f32[]{:T(128)} %get-tuple-element.306, f32[]{:T(128)} %get-tuple-element.303), kind=kOutput, calls=%fused_computation.4.clone.1 | convolution fusion | flops 1813118976 | bytes 5505032 | tf_op jit(solution)/shard_map/while/body/eval_jaxpr/while/body/dot_general | solution.py:18
  228.6 3.7 %fusion.38 = f32[768,256]{0,1:T(8,128)S(1)} fusion(f32[768,256]{0,1:T(8,128)S(1)} %copy.48, f32[768,256]{0,1:T(8,128)} %get-tuple-element.307, f32[768,768]{1,0:T(8,128)S(1)} %get-tuple-element.305, f32[768,256]{0,1:T(8,128)} %get-tuple-element.304, f32[]{:T(128)} %get-tuple-element.306, f32[]{:T(128)} %get-tuple-element.303), kind=kOutput, calls=%fused_computation.4.clone.1 | convolution fusion | flops 1813118976 | bytes 5505032 | tf_op jit(solution)/shard_map/while/body/eval_jaxpr/while/body/dot_general | solution.py:18
  233.0 3.7 %fusion.38 = f32[768,256]{0,1:T(8,128)S(1)} fusion(f32[768,256]{0,1:T(8,128)S(1)} %copy.48, f32[768,256]{0,1:T(8,128)} %get-tuple-element.307, f32[768,768]{1,0:T(8,128)S(1)} %get-tuple-element.305, f32[768,256]{0,1:T(8,128)} %get-tuple-element.304, f32[]{:T(128)} %get-tuple-element.306, f32[]{:T(128)} %get-tuple-element.303), kind=kOutput, calls=%fused_computation.4.clone.1 | convolution fusion | flops 1813118976 | bytes 5505032 | tf_op jit(solution)/shard_map/while/body/eval_jaxpr/while/body/dot_general | solution.py:18
  237.3 2.9 fusion.34
  246.0 11.4 %psum.14 = f32[2]{0:T(128)S(1)} all-reduce(f32[2]{0:T(128)S(1)} %compare_select_fusion), channel_id=1, replica_groups=mesh['expert'=8,'token'=4] {'token'}, use_global_device_ids=true, to_apply=%region_8.9 | all-reduce | flops 2 | bytes 16 | tf_op jit(solution)/shard_map/psum | solution.py:56
  257.4 55.3 %psum.15 = f32[]{:T(128)} all-reduce(f32[]{:T(128)} %reduce_sum.47), channel_id=1, replica_groups=mesh['expert'=8,'token'=4] {'expert','token'}, use_global_device_ids=true, to_apply=%region_10.11 | all-reduce | flops 1 | bytes 8 | tf_op jit(solution)/shard_map/psum | solution.py:57
  (96 shorter events, 71.4 us)
Async XLA Ops:
  7.2 69.2 %all-gather.2.cloned.1.call-start = ((), (), s32[]{:S(2)}) async-start(), calls=%async_computation | async-start | bytes 3932160 | tf_op jit(solution)/shard_map/all_gather | solution.py:40
  10.1 71.0 %copy-start.1 = (s32[4]{0:T(128)S(1)}, s32[4]{0:T(128)}, u32[]{:S(2)}) copy-start(s32[4]{0:T(128)} %param.14) | copy-start | bytes 52
  10.1 71.0 %copy-start.2 = (f32[4]{0:T(128)S(1)}, f32[4]{0:T(128)}, u32[]{:S(2)}) copy-start(f32[4]{0:T(128)} %param.15) | copy-start | bytes 52
  91.6 0.9 copy-start
  138.9 0.9 copy-start
  186.3 0.9 copy-start
  220.4 0.9 copy-start
Sparse Core Ops, SparseCore 0:
  10.2 66.1 all-gather.1
where the time goes:
time: 323 us; the launch traced here: 321 us
  matrix products  90.8 us (28%)
  blocking collectives  66.7 us (21%)
  waiting for transfers between devices  66.3 us (21%)
  local copies, waits for them, and re-layouts  47.1 us (15%)
  other arithmetic  17.6 us (5%)
  loops' own time  16.9 us (5%)
  between operations  15.4 us (5%)
    dot_general x18, matrix products, advance(): jnp.dot(gram_matrix, current - float_weights, precision=lax.Precision.HIG...  66.3 us
    all_gather x1, waiting for transfers between devices, on_device(): lax.all_gather(masked, 'token', axis=1, tiled=True)  66.2 us
    psum x1, blocking collectives, on_device(): layer_energy = lax.psum(jnp.sum(energies), ('expert', 'token'))  55.3 us
    dynamic_slice x24, local copies, waits for them, and re-layouts, on_device(): lax.map(one_task, (weights, kept_mask, step_counts, ridge_scale))  23.4 us
    dynamic_update_slice x16, local copies, waits for them, and re-layouts, on_device(): lax.map(one_task, (weights, kept_mask, step_counts, ridge_scale))  19.2 us
    another operation x4, loops' own time, solve_task(): result = lax.fori_loop(0, task_count, advance, float_mask * float_weights)  14.3 us
    dot_general x4, matrix products, solve_task(): jnp.dot(gram_matrix, change, precision=lax.Precision.HIGHEST)  11.5 us
    psum x1, blocking collectives, on_device(): expert_terms = lax.psum(picker * jnp.sum(numerators), 'token')  11.4 us
  transfers between devices with their start and end apart: 1, of which 1 were waited for; matrix products, arithmetic and copies ran while one was open for 0% of the time, Pallas kernels for 0%

commit v1 on v0

--- a/solution.py
+++ b/solution.py
@@ -5,6 +5,27 @@
 
 D = 2048
 COLS = 256
+
+
+def gather_around(x, axis, dim):
+    size, index, rows = (lax.axis_size(axis), lax.axis_index(axis), x.shape[dim])
+    ahead = [(i, (i + 1) % size) for i in range(size)]
+    backward = [(i, (i - 1) % size) for i in range(size)]
+    filled = jnp.zeros((*x.shape[:dim], size * rows, *x.shape[dim + 1 :]), x.dtype)
+    filled = lax.dynamic_update_slice_in_dim(filled, x, index * rows, axis=dim)
+    from_left = from_right = x
+    half = size // 2
+    for step in range(1, half + 1):
+        from_left = lax.ppermute(from_left, axis, ahead)
+        filled = lax.dynamic_update_slice_in_dim(
+            filled, from_left, (index - step) % size * rows, axis=dim
+        )
+        if step < size - half:
+            from_right = lax.ppermute(from_right, axis, backward)
+            filled = lax.dynamic_update_slice_in_dim(
+                filled, from_right, (index + step) % size * rows, axis=dim
+            )
+    return filled
 
 
 def solve_task(gram_matrix, frobenius, task_weights, task_mask, task_count, task_ridge):
@@ -37,7 +58,7 @@
     own_slot = lax.axis_index("token") * local_tasks // per_expert
     masked = activations * routed[:, :, None].astype(jnp.bfloat16)
     own_rows = lax.dynamic_index_in_dim(
-        lax.all_gather(masked, "token", axis=1, tiled=True), own_slot, 0, keepdims=False
+        gather_around(masked, "token", 1), own_slot, 0, keepdims=False
     )
     gram_sum = lax.dot_general(
         own_rows, own_rows, (((0,), (0,)), ((), ())), preferred_element_type=jnp.float32

time: 323 us -> 301 us (0.932)
  waiting for transfers between devices: 66.3 us -> 49.3 us
  between operations: 15.4 us -> 1.92 us
  starting transfers between devices: 0.04 us -> 5.15 us
  local copies, waits for them, and re-layouts: 47.1 us -> 51.9 us
    all_gather x1 -> x0, waiting for transfers between devices: 66.2 us -> none  [on_device(): lax.all_gather(masked, 'token', axis=1, tiled=True)]
    ppermute x0 -> x3, waiting for transfers between devices: none -> 49.3 us  [the longest x2 34.8 us: gather_around(): from_left = lax.ppermute(from_left, axis, ahead)]
    ppermute x0 -> x3, starting transfers between devices: none -> 5.15 us  [the longest x2 3.08 us: gather_around(): from_left = lax.ppermute(from_left, axis, ahead)]
  transfers between devices with their start and end apart: 1 -> 3, of which waited for: 1 -> 3; matrix products, arithmetic and copies ran while one was open for 0% -> 1% of each run, Pallas kernels for 0% -> 0%
where the time goes in v1:
time: 301 us; the launch traced here: 299 us
  matrix products  90.8 us (30%)
  blocking collectives  66.7 us (22%)
  local copies, waits for them, and re-layouts  51.9 us (17%)
  waiting for transfers between devices  49.3 us (16%)
  loops' own time  16.9 us (6%)
  other arithmetic  16.6 us (6%)
  starting transfers between devices  5.15 us (2%)
    dot_general x18, matrix products, advance(): jnp.dot(gram_matrix, current - float_weights, precision=lax.Precision.HIG...  66.3 us
    psum x1, blocking collectives, on_device(): layer_energy = lax.psum(jnp.sum(energies), ('expert', 'token'))  55.8 us
    ppermute x2, waiting for transfers between devices, gather_around(): from_left = lax.ppermute(from_left, axis, ahead)  34.8 us
    dynamic_slice x24, local copies, waits for them, and re-layouts, on_device(): lax.map(one_task, (weights, kept_mask, step_counts, ridge_scale))  23.4 us
    dynamic_update_slice x16, local copies, waits for them, and re-layouts, on_device(): lax.map(one_task, (weights, kept_mask, step_counts, ridge_scale))  19.2 us
    ppermute x1, waiting for transfers between devices, gather_around(): from_right = lax.ppermute(from_right, axis, backward)  14.6 us
    another operation x4, loops' own time, solve_task(): result = lax.fori_loop(0, task_count, advance, float_mask * float_weights)  14.3 us
    dot_general x4, matrix products, solve_task(): jnp.dot(gram_matrix, change, precision=lax.Precision.HIGHEST)  11.5 us
  transfers between devices with their start and end apart: 3, of which 3 were waited for; matrix products, arithmetic and copies ran while one was open for 1% of the time, Pallas kernels for 0%

profile of v1, /device:TPU:0, one launch (start us, length us, event | category | flops | bytes accessed | tf_op | source)
XLA Modules:
  0.0 299.2 jit_solution(4611825249701073098)
XLA Ops:
  4.3 3.1 %collective-permute-start = (bf16[2,256,768]{2,1,0:T(8,128)(2,1)S(1)}, bf16[2,256,768]{2,1,0:T(8,128)(2,1)S(1)}, u32[]{:S(2)}, u32[]{:S(2)}) collective-permute-start(bf16[2,256,768]{2,1,0:T(8,128)(2,1)S(1)} %get-tuple-element.151), channel_id=1, source_target_pairs={{0,1},{1,2},{2,3},{3,0},{4,5},{5,6},{6,7},{7,4},{8,9},{9,10},{10,1... | collective-permute-start | bytes 2359304 | tf_op jit(solution)/shard_map/ppermute | solution.py:19
  9.5 18.4 %collective-permute-done = bf16[2,256,768]{2,1,0:T(8,128)(2,1)S(1)} collective-permute-done((bf16[2,256,768]{2,1,0:T(8,128)(2,1)S(1)}, bf16[2,256,768]{2,1,0:T(8,128)(2,1)S(1)}, u32[]{:S(2)}, u32[]{:S(2)}) %collective-permute-start) | collective-permute-done | bytes 786464 | tf_op jit(solution)/shard_map/ppermute | solution.py:19
  28.9 14.6 %collective-permute-done.1 = bf16[2,256,768]{2,1,0:T(8,128)(2,1)S(1)} collective-permute-done((bf16[2,256,768]{2,1,0:T(8,128)(2,1)S(1)}, bf16[2,256,768]{2,1,0:T(8,128)(2,1)S(1)}, u32[]{:S(2)}, u32[]{:S(2)}) %collective-permute-start.1) | collective-permute-done | bytes 786464 | tf_op jit(solution)/shard_map/ppermute | solution.py:24
  44.4 16.4 %collective-permute-done.2 = bf16[2,256,768]{2,1,0:T(8,128)(2,1)S(1)} collective-permute-done((bf16[2,256,768]{2,1,0:T(8,128)(2,1)S(1)}, bf16[2,256,768]{2,1,0:T(8,128)(2,1)S(1)}, u32[]{:S(2)}, u32[]{:S(2)}) %collective-permute-start.2) | collective-permute-done | bytes 786464 | tf_op jit(solution)/shard_map/ppermute | solution.py:19
  61.7 4.1 %multiply_reduce_fusion = (f32[]{:T(128)}, f32[768,768]{1,0:T(8,128)S(1)}) fusion(bf16[2,1024,768]{2,1,0:T(8,128)(2,1)} %constant_dynamic-update-slice_fusion.1, s32[]{:T(128)S(6)} %select_n.43), kind=kOutput, calls=%fused_computation.22 | convolution fusion | flops 1209729024 | bytes 3932168 | tf_op jit(solution)/shard_map/dot_general | solution.py:63
  66.4 163.0 %while.25 = (s32[]{:T(128)}, f32[4,768,256]{2,1,0:T(8,128)}, f32[4]{0:T(128)S(1)}, f32[4]{0:T(128)S(1)}, s32[4,768,256]{2,1,0:T(8,128)}, /*index=5*/bf16[4,768,2...) while((s32[]{:T(128)}, f32[4,768,256]{2,1,0:T(8,128)}, ...), condition=%wide.region_6.7_spmd, body=%wide.region_1.6_spmd.sunk | while | flops 5439750144 | bytes 29491652 | solution.py:73
  79.9 27.0 %while.26 = (s32[]{:T(128)}, f32[768,256]{0,1:T(8,128)S(1)}, s32[]{:T(128)}, f32[]{:T(128)}, f32[768,256]{0,1:T(8,128)}, /*index=5*/f32[768,768]{1,0:T(8,128)S(1)}, f32[]{:T(128)}, f32[768,256]{0,1:T(8,128)}, s32[]{:T(128)}) while((s32[]{:T(128)}, f32[768,256]{0,1:T(8,128)S(1)}, s32[]{:T(128)}, f32[]{:T(128)}, f32[768,256]{0,1:T(8,128)}, ...), condition=%wide.region_3.3_spmd, body=%wide.region_2.2_spmd.sunk | while | flops 1813118976 | bytes 7077989 | solution.py:44
  80.6 3.7 %fusion.38 = f32[768,256]{0,1:T(8,128)S(1)} fusion(f32[768,256]{0,1:T(8,128)S(1)} %copy.52, f32[768,256]{0,1:T(8,128)} %get-tuple-element.309, f32[768,768]{1,0:T(8,128)S(1)} %get-tuple-element.307, f32[768,256]{0,1:T(8,128)} %get-tuple-element.306, f32[]{:T(128)} %get-tuple-element.308, f32[]{:T(128)} %get-tuple-element.305), kind=kOutput, calls=%fused_computation.4.clone.1 | convolution fusion | flops 1813118976 | bytes 5505032 | tf_op jit(solution)/shard_map/while/body/eval_jaxpr/while/body/dot_general | solution.py:39
  85.0 3.7 %fusion.38 = f32[768,256]{0,1:T(8,128)S(1)} fusion(f32[768,256]{0,1:T(8,128)S(1)} %copy.52, f32[768,256]{0,1:T(8,128)} %get-tuple-element.309, f32[768,768]{1,0:T(8,128)S(1)} %get-tuple-element.307, f32[768,256]{0,1:T(8,128)} %get-tuple-element.306, f32[]{:T(128)} %get-tuple-element.308, f32[]{:T(128)} %get-tuple-element.305), kind=kOutput, calls=%fused_computation.4.clone.1 | convolution fusion | flops 1813118976 | bytes 5505032 | tf_op jit(solution)/shard_map/while/body/eval_jaxpr/while/body/dot_general | solution.py:39
  89.4 3.7 %fusion.38 = f32[768,256]{0,1:T(8,128)S(1)} fusion(f32[768,256]{0,1:T(8,128)S(1)} %copy.52, f32[768,256]{0,1:T(8,128)} %get-tuple-element.309, f32[768,768]{1,0:T(8,128)S(1)} %get-tuple-element.307, f32[768,256]{0,1:T(8,128)} %get-tuple-element.306, f32[]{:T(128)} %get-tuple-element.308, f32[]{:T(128)} %get-tuple-element.305), kind=kOutput, calls=%fused_computation.4.clone.1 | convolution fusion | flops 1813118976 | bytes 5505032 | tf_op jit(solution)/shard_map/while/body/eval_jaxpr/while/body/dot_general | solution.py:39
  93.8 3.7 %fusion.38 = f32[768,256]{0,1:T(8,128)S(1)} fusion(f32[768,256]{0,1:T(8,128)S(1)} %copy.52, f32[768,256]{0,1:T(8,128)} %get-tuple-element.309, f32[768,768]{1,0:T(8,128)S(1)} %get-tuple-element.307, f32[768,256]{0,1:T(8,128)} %get-tuple-element.306, f32[]{:T(128)} %get-tuple-element.308, f32[]{:T(128)} %get-tuple-element.305), kind=kOutput, calls=%fused_computation.4.clone.1 | convolution fusion | flops 1813118976 | bytes 5505032 | tf_op jit(solution)/shard_map/while/body/eval_jaxpr/while/body/dot_general | solution.py:39
  98.2 3.7 %fusion.38 = f32[768,256]{0,1:T(8,128)S(1)} fusion(f32[768,256]{0,1:T(8,128)S(1)} %copy.52, f32[768,256]{0,1:T(8,128)} %get-tuple-element.309, f32[768,768]{1,0:T(8,128)S(1)} %get-tuple-element.307, f32[768,256]{0,1:T(8,128)} %get-tuple-element.306, f32[]{:T(128)} %get-tuple-element.308, f32[]{:T(128)} %get-tuple-element.305), kind=kOutput, calls=%fused_computation.4.clone.1 | convolution fusion | flops 1813118976 | bytes 5505032 | tf_op jit(solution)/shard_map/while/body/eval_jaxpr/while/body/dot_general | solution.py:39
  102.6 3.7 %fusion.38 = f32[768,256]{0,1:T(8,128)S(1)} fusion(f32[768,256]{0,1:T(8,128)S(1)} %copy.52, f32[768,256]{0,1:T(8,128)} %get-tuple-element.309, f32[768,768]{1,0:T(8,128)S(1)} %get-tuple-element.307, f32[768,256]{0,1:T(8,128)} %get-tuple-element.306, f32[]{:T(128)} %get-tuple-element.308, f32[]{:T(128)} %get-tuple-element.305), kind=kOutput, calls=%fused_computation.4.clone.1 | convolution fusion | flops 1813118976 | bytes 5505032 | tf_op jit(solution)/shard_map/while/body/eval_jaxpr/while/body/dot_general | solution.py:39
  127.3 27.0 %while.26 = (s32[]{:T(128)}, f32[768,256]{0,1:T(8,128)S(1)}, s32[]{:T(128)}, f32[]{:T(128)}, f32[768,256]{0,1:T(8,128)}, /*index=5*/f32[768,768]{1,0:T(8,128)S(1)}, f32[]{:T(128)}, f32[768,256]{0,1:T(8,128)}, s32[]{:T(128)}) while((s32[]{:T(128)}, f32[768,256]{0,1:T(8,128)S(1)}, s32[]{:T(128)}, f32[]{:T(128)}, f32[768,256]{0,1:T(8,128)}, ...), condition=%wide.region_3.3_spmd, body=%wide.region_2.2_spmd.sunk | while | flops 1813118976 | bytes 7077989 | solution.py:44
  128.0 3.7 %fusion.38 = f32[768,256]{0,1:T(8,128)S(1)} fusion(f32[768,256]{0,1:T(8,128)S(1)} %copy.52, f32[768,256]{0,1:T(8,128)} %get-tuple-element.309, f32[768,768]{1,0:T(8,128)S(1)} %get-tuple-element.307, f32[768,256]{0,1:T(8,128)} %get-tuple-element.306, f32[]{:T(128)} %get-tuple-element.308, f32[]{:T(128)} %get-tuple-element.305), kind=kOutput, calls=%fused_computation.4.clone.1 | convolution fusion | flops 1813118976 | bytes 5505032 | tf_op jit(solution)/shard_map/while/body/eval_jaxpr/while/body/dot_general | solution.py:39
  132.4 3.7 %fusion.38 = f32[768,256]{0,1:T(8,128)S(1)} fusion(f32[768,256]{0,1:T(8,128)S(1)} %copy.52, f32[768,256]{0,1:T(8,128)} %get-tuple-element.309, f32[768,768]{1,0:T(8,128)S(1)} %get-tuple-element.307, f32[768,256]{0,1:T(8,128)} %get-tuple-element.306, f32[]{:T(128)} %get-tuple-element.308, f32[]{:T(128)} %get-tuple-element.305), kind=kOutput, calls=%fused_computation.4.clone.1 | convolution fusion | flops 1813118976 | bytes 5505032 | tf_op jit(solution)/shard_map/while/body/eval_jaxpr/while/body/dot_general | solution.py:39
  136.8 3.7 %fusion.38 = f32[768,256]{0,1:T(8,128)S(1)} fusion(f32[768,256]{0,1:T(8,128)S(1)} %copy.52, f32[768,256]{0,1:T(8,128)} %get-tuple-element.309, f32[768,768]{1,0:T(8,128)S(1)} %get-tuple-element.307, f32[768,256]{0,1:T(8,128)} %get-tuple-element.306, f32[]{:T(128)} %get-tuple-element.308, f32[]{:T(128)} %get-tuple-element.305), kind=kOutput, calls=%fused_computation.4.clone.1 | convolution fusion | flops 1813118976 | bytes 5505032 | tf_op jit(solution)/shard_map/while/body/eval_jaxpr/while/body/dot_general | solution.py:39
  141.2 3.7 %fusion.38 = f32[768,256]{0,1:T(8,128)S(1)} fusion(f32[768,256]{0,1:T(8,128)S(1)} %copy.52, f32[768,256]{0,1:T(8,128)} %get-tuple-element.309, f32[768,768]{1,0:T(8,128)S(1)} %get-tuple-element.307, f32[768,256]{0,1:T(8,128)} %get-tuple-element.306, f32[]{:T(128)} %get-tuple-element.308, f32[]{:T(128)} %get-tuple-element.305), kind=kOutput, calls=%fused_computation.4.clone.1 | convolution fusion | flops 1813118976 | bytes 5505032 | tf_op jit(solution)/shard_map/while/body/eval_jaxpr/while/body/dot_general | solution.py:39
  145.5 3.7 %fusion.38 = f32[768,256]{0,1:T(8,128)S(1)} fusion(f32[768,256]{0,1:T(8,128)S(1)} %copy.52, f32[768,256]{0,1:T(8,128)} %get-tuple-element.309, f32[768,768]{1,0:T(8,128)S(1)} %get-tuple-element.307, f32[768,256]{0,1:T(8,128)} %get-tuple-element.306, f32[]{:T(128)} %get-tuple-element.308, f32[]{:T(128)} %get-tuple-element.305), kind=kOutput, calls=%fused_computation.4.clone.1 | convolution fusion | flops 1813118976 | bytes 5505032 | tf_op jit(solution)/shard_map/while/body/eval_jaxpr/while/body/dot_general | solution.py:39
  149.9 3.7 %fusion.38 = f32[768,256]{0,1:T(8,128)S(1)} fusion(f32[768,256]{0,1:T(8,128)S(1)} %copy.52, f32[768,256]{0,1:T(8,128)} %get-tuple-element.309, f32[768,768]{1,0:T(8,128)S(1)} %get-tuple-element.307, f32[768,256]{0,1:T(8,128)} %get-tuple-element.306, f32[]{:T(128)} %get-tuple-element.308, f32[]{:T(128)} %get-tuple-element.305), kind=kOutput, calls=%fused_computation.4.clone.1 | convolution fusion | flops 1813118976 | bytes 5505032 | tf_op jit(solution)/shard_map/while/body/eval_jaxpr/while/body/dot_general | solution.py:39
  154.3 2.9 fusion.34
  174.6 13.8 %while.26 = (s32[]{:T(128)}, f32[768,256]{0,1:T(8,128)S(1)}, s32[]{:T(128)}, f32[]{:T(128)}, f32[768,256]{0,1:T(8,128)}, /*index=5*/f32[768,768]{1,0:T(8,128)S(1)}, f32[]{:T(128)}, f32[768,256]{0,1:T(8,128)}, s32[]{:T(128)}) while((s32[]{:T(128)}, f32[768,256]{0,1:T(8,128)S(1)}, s32[]{:T(128)}, f32[]{:T(128)}, f32[768,256]{0,1:T(8,128)}, ...), condition=%wide.region_3.3_spmd, body=%wide.region_2.2_spmd.sunk | while | flops 1813118976 | bytes 7077989 | solution.py:44
  175.3 3.7 %fusion.38 = f32[768,256]{0,1:T(8,128)S(1)} fusion(f32[768,256]{0,1:T(8,128)S(1)} %copy.52, f32[768,256]{0,1:T(8,128)} %get-tuple-element.309, f32[768,768]{1,0:T(8,128)S(1)} %get-tuple-element.307, f32[768,256]{0,1:T(8,128)} %get-tuple-element.306, f32[]{:T(128)} %get-tuple-element.308, f32[]{:T(128)} %get-tuple-element.305), kind=kOutput, calls=%fused_computation.4.clone.1 | convolution fusion | flops 1813118976 | bytes 5505032 | tf_op jit(solution)/shard_map/while/body/eval_jaxpr/while/body/dot_general | solution.py:39
  179.7 3.7 %fusion.38 = f32[768,256]{0,1:T(8,128)S(1)} fusion(f32[768,256]{0,1:T(8,128)S(1)} %copy.52, f32[768,256]{0,1:T(8,128)} %get-tuple-element.309, f32[768,768]{1,0:T(8,128)S(1)} %get-tuple-element.307, f32[768,256]{0,1:T(8,128)} %get-tuple-element.306, f32[]{:T(128)} %get-tuple-element.308, f32[]{:T(128)} %get-tuple-element.305), kind=kOutput, calls=%fused_computation.4.clone.1 | convolution fusion | flops 1813118976 | bytes 5505032 | tf_op jit(solution)/shard_map/while/body/eval_jaxpr/while/body/dot_general | solution.py:39
  184.1 3.7 %fusion.38 = f32[768,256]{0,1:T(8,128)S(1)} fusion(f32[768,256]{0,1:T(8,128)S(1)} %copy.52, f32[768,256]{0,1:T(8,128)} %get-tuple-element.309, f32[768,768]{1,0:T(8,128)S(1)} %get-tuple-element.307, f32[768,256]{0,1:T(8,128)} %get-tuple-element.306, f32[]{:T(128)} %get-tuple-element.308, f32[]{:T(128)} %get-tuple-element.305), kind=kOutput, calls=%fused_computation.4.clone.1 | convolution fusion | flops 1813118976 | bytes 5505032 | tf_op jit(solution)/shard_map/while/body/eval_jaxpr/while/body/dot_general | solution.py:39
  208.8 13.8 %while.26 = (s32[]{:T(128)}, f32[768,256]{0,1:T(8,128)S(1)}, s32[]{:T(128)}, f32[]{:T(128)}, f32[768,256]{0,1:T(8,128)}, /*index=5*/f32[768,768]{1,0:T(8,128)S(1)}, f32[]{:T(128)}, f32[768,256]{0,1:T(8,128)}, s32[]{:T(128)}) while((s32[]{:T(128)}, f32[768,256]{0,1:T(8,128)S(1)}, s32[]{:T(128)}, f32[]{:T(128)}, f32[768,256]{0,1:T(8,128)}, ...), condition=%wide.region_3.3_spmd, body=%wide.region_2.2_spmd.sunk | while | flops 1813118976 | bytes 7077989 | solution.py:44
  209.5 3.7 %fusion.38 = f32[768,256]{0,1:T(8,128)S(1)} fusion(f32[768,256]{0,1:T(8,128)S(1)} %copy.52, f32[768,256]{0,1:T(8,128)} %get-tuple-element.309, f32[768,768]{1,0:T(8,128)S(1)} %get-tuple-element.307, f32[768,256]{0,1:T(8,128)} %get-tuple-element.306, f32[]{:T(128)} %get-tuple-element.308, f32[]{:T(128)} %get-tuple-element.305), kind=kOutput, calls=%fused_computation.4.clone.1 | convolution fusion | flops 1813118976 | bytes 5505032 | tf_op jit(solution)/shard_map/while/body/eval_jaxpr/while/body/dot_general | solution.py:39
  213.9 3.7 %fusion.38 = f32[768,256]{0,1:T(8,128)S(1)} fusion(f32[768,256]{0,1:T(8,128)S(1)} %copy.52, f32[768,256]{0,1:T(8,128)} %get-tuple-element.309, f32[768,768]{1,0:T(8,128)S(1)} %get-tuple-element.307, f32[768,256]{0,1:T(8,128)} %get-tuple-element.306, f32[]{:T(128)} %get-tuple-element.308, f32[]{:T(128)} %get-tuple-element.305), kind=kOutput, calls=%fused_computation.4.clone.1 | convolution fusion | flops 1813118976 | bytes 5505032 | tf_op jit(solution)/shard_map/while/body/eval_jaxpr/while/body/dot_general | solution.py:39
  218.3 3.7 %fusion.38 = f32[768,256]{0,1:T(8,128)S(1)} fusion(f32[768,256]{0,1:T(8,128)S(1)} %copy.52, f32[768,256]{0,1:T(8,128)} %get-tuple-element.309, f32[768,768]{1,0:T(8,128)S(1)} %get-tuple-element.307, f32[768,256]{0,1:T(8,128)} %get-tuple-element.306, f32[]{:T(128)} %get-tuple-element.308, f32[]{:T(128)} %get-tuple-element.305), kind=kOutput, calls=%fused_computation.4.clone.1 | convolution fusion | flops 1813118976 | bytes 5505032 | tf_op jit(solution)/shard_map/while/body/eval_jaxpr/while/body/dot_general | solution.py:39
  222.6 2.9 fusion.34
  231.3 11.0 %psum.14 = f32[2]{0:T(128)S(1)} all-reduce(f32[2]{0:T(128)S(1)} %compare_select_fusion), channel_id=1, replica_groups=mesh['expert'=8,'token'=4] {'token'}, use_global_device_ids=true, to_apply=%region_8.9 | all-reduce | flops 2 | bytes 16 | tf_op jit(solution)/shard_map/psum | solution.py:77
  242.3 55.8 %psum.15 = f32[]{:T(128)} all-reduce(f32[]{:T(128)} %reduce_sum.47), channel_id=1, replica_groups=mesh['expert'=8,'token'=4] {'expert','token'}, use_global_device_ids=true, to_apply=%region_10.11 | all-reduce | flops 1 | bytes 8 | tf_op jit(solution)/shard_map/psum | solution.py:78
  (105 shorter events, 85.1 us)
Async XLA Ops:
  0.6 2.6 copy-start.1
  4.3 23.6 %collective-permute-start = (bf16[2,256,768]{2,1,0:T(8,128)(2,1)S(1)}, bf16[2,256,768]{2,1,0:T(8,128)(2,1)S(1)}, u32[]{:S(2)}, u32[]{:S(2)}) collective-permute-start(bf16[2,256,768]{2,1,0:T(8,128)(2,1)S(1)} %get-tuple-element.151), channel_id=1, source_target_pairs={{0,1},{1,2},{2,3},{3,0},{4,5},{5,6},{6,7},{7,4},{8,9},{9,10},{10,1... | collective-permute-start | bytes 2359304 | tf_op jit(solution)/shard_map/ppermute | solution.py:19
  7.4 36.1 %collective-permute-start.1 = (bf16[2,256,768]{2,1,0:T(8,128)(2,1)S(1)}, bf16[2,256,768]{2,1,0:T(8,128)(2,1)S(1)}, u32[]{:S(2)}, u32[]{:S(2)}) collective-permute-start(bf16[2,256,768]{2,1,0:T(8,128)(2,1)S(1)} %get-tuple-element.151), channel_id=1, source_target_pairs={{0,3},{1,0},{2,1},{3,2},{4,7},{5,4},{6,5},{7,6},{8,11},{9,8},{10,9... | collective-permute-start | bytes 2359304 | tf_op jit(solution)/shard_map/ppermute | solution.py:24
  27.9 32.8 %collective-permute-start.2 = (bf16[2,256,768]{2,1,0:T(8,128)(2,1)S(1)}, bf16[2,256,768]{2,1,0:T(8,128)(2,1)S(1)}, u32[]{:S(2)}, u32[]{:S(2)}) collective-permute-start(bf16[2,256,768]{2,1,0:T(8,128)(2,1)S(1)} %collective-permute-done), channel_id=1, source_target_pairs={{0,1},{1,2},{2,3},{3,0},{4,5},{5,6},{6,7},{7,4},{8,9},{9,10},{10,1... | collective-permute-start | bytes 2359304 | tf_op jit(solution)/shard_map/ppermute | solution.py:19
  44.4 22.0 %copy-start.2 = (s32[4]{0:T(128)S(1)}, s32[4]{0:T(128)}, u32[]{:S(2)}) copy-start(s32[4]{0:T(128)} %param.14) | copy-start | bytes 52
  44.4 22.0 %copy-start.3 = (f32[4]{0:T(128)S(1)}, f32[4]{0:T(128)}, u32[]{:S(2)}) copy-start(f32[4]{0:T(128)} %param.15) | copy-start | bytes 52
  76.9 0.9 copy-start
  124.2 0.9 copy-start
  171.6 0.9 copy-start
  205.7 0.9 copy-start
